TPU v7x, 256 devices: a whole 4x4x8 slice. The times are simulated.
256 devices in a mesh: dp: 8 (over y, core), expert: 32 (over x, z).
Axes of the slice: x: 4, y: 4, z: 8, core: 2. Of those that a mesh axis runs over, the one named last changes fastest.
Arguments:
- tokens: bfloat16 [2048, 4096], P(('dp', 'expert')), may hold values from -6 to 6
- expert_ids: int32 [2048, 8], P(('dp', 'expert')), may hold values from 0 to 31, all different within a row; in each aligned block of 8 rows (0 to 7, 8 to 15, ...) at most 3 rows name the same one
- gate_values: float32 [2048, 8], P(('dp', 'expert')), may hold values from 0.05 to 1
- w_gate: bfloat16 [32, 4096, 2048], P('expert', None, 'dp'), may hold values from -0.09375 to 0.09375
- w_up: bfloat16 [32, 4096, 2048], P('expert', None, 'dp'), may hold values from -0.09375 to 0.09375
- w_down: bfloat16 [32, 2048, 4096], P('expert', 'dp'), may hold values from -0.125 to 0.125
- s_gate: bfloat16 [4096, 2048], P(None, 'dp'), may hold values from -0.09375 to 0.09375
- s_up: bfloat16 [4096, 2048], P(None, 'dp'), may hold values from -0.09375 to 0.09375
- s_down: bfloat16 [2048, 4096], P('dp'), may hold values from -0.125 to 0.125
Outputs:
- mixed: bfloat16 [2048, 4096], P(('dp', 'expert'))
Inputs may be any that keep to these rules, and one draw needn't show every extreme that they name: `expert_ids`: each row names 8 different experts; the 8 rows of one device name one expert at most 3 times.
All inputs are finite; a program needn't handle non-finite values.
Results may differ from a plain program's by a relative error of at most 0.0054.
Values may be sent and summed in bfloat16 or wider, within the bound.
No kernel may reach another device: no remote copies, remote signals or barrier semaphores. Data moves between devices by JAX's collectives and lax.ppermute only.
A program may use at most 128 MiB of HBM per device.

v0:
```python
import jax
import jax.numpy as jnp
from jax import lax
from jax.sharding import PartitionSpec as P


def swiglu(rows, gate_w, up_w, down_w):
    gate = jnp.dot(rows, gate_w, preferred_element_type=jnp.float32)
    up = jnp.dot(rows, up_w, preferred_element_type=jnp.float32)
    hidden = (jax.nn.silu(gate) * up).astype(jnp.bfloat16)
    return jnp.dot(hidden, down_w, preferred_element_type=jnp.float32)


def slot_tables(route_ids, route_gates, experts, capacity):
    row_count, picks = route_ids.shape
    listed = route_ids.reshape(-1)
    expert_range = jnp.arange(experts, dtype=jnp.int32)
    marks = (listed[:, None] == expert_range[None, :]).astype(jnp.int32)
    earlier = jnp.cumsum(marks, axis=0) - marks
    position = jnp.sum(earlier * marks, axis=1)
    slot_index = (listed * capacity + position).reshape(row_count, picks)
    slot_range = jnp.arange(experts * capacity, dtype=jnp.int32)
    matches = slot_index[:, :, None] == slot_range[None, None, :]
    picker = jnp.any(matches, axis=1).astype(jnp.bfloat16)
    combiner = jnp.sum(jnp.where(matches, route_gates[:, :, None], jnp.float32(0.0)), axis=1)
    return (picker, combiner)


def dispatch_rows(picker, source_rows):
    placed = jnp.einsum("rs,rd->sd", picker, source_rows, preferred_element_type=jnp.float32)
    return placed.astype(jnp.bfloat16)


def per_device(tokens, expert_ids, gate_values, w_gate, w_up, w_down, s_gate, s_up, s_down):
    experts = lax.axis_size("expert")
    groups = lax.axis_size("dp")
    own_rows, width = tokens.shape
    picks = expert_ids.shape[1]
    capacity = max(2, min(own_rows, 3 * own_rows * picks // (2 * experts)))
    gate_local = w_gate[0]
    up_local = w_up[0]
    down_local = w_down[0]
    column = lax.all_gather(tokens, "dp", axis=0, tiled=True)
    column_ids, column_gates = (
        lax.all_gather(expert_ids, "dp", axis=0, tiled=True),
        lax.all_gather(gate_values, "dp", axis=0, tiled=True),
    )
    column_cap = capacity * groups
    picker, combiner = slot_tables(column_ids, column_gates, experts, column_cap)
    outgoing = dispatch_rows(picker, column).reshape(experts, column_cap, width)
    arrived = lax.all_to_all(outgoing, "expert", split_axis=0, concat_axis=0, tiled=True)
    items = arrived.shape[1]
    partial_value = swiglu(
        arrived.reshape(experts * items, width), gate_local, up_local, down_local
    )
    partial_value = partial_value.astype(jnp.bfloat16).reshape(experts, items, width)
    returned = lax.all_to_all(partial_value, "expert", split_axis=0, concat_axis=0, tiled=True)
    returned_rows = returned.reshape(experts * column_cap, width)
    routed = jnp.dot(
        combiner,
        returned_rows.astype(jnp.float32),
        precision=lax.Precision.HIGHEST,
        preferred_element_type=jnp.float32,
    )
    mixed = lax.psum_scatter(
        swiglu(column, s_gate, s_up, s_down) + routed, "dp", scatter_dimension=0, tiled=True
    )
    return mixed.astype(jnp.bfloat16)


def solution(mesh):
    placed = (
        P(("dp", "expert"), None),
        P(("dp", "expert"), None),
        P(("dp", "expert"), None),
        P("expert", None, "dp"),
        P("expert", None, "dp"),
        P("expert", "dp", None),
        P(None, "dp"),
        P(None, "dp"),
        P("dp", None),
    )
    return jax.shard_map(
        per_device, mesh=mesh, in_specs=placed, out_specs=P(("dp", "expert"), None), check_vma=False
    )
```

profile of v0, /device:TPU:2, one launch (start us, length us, event | category | flops | bytes accessed | tf_op | source)
XLA Modules:
  0.0 403.5 jit_solution(12211258155983552361)
XLA Ops:
  6.5 0.0 copy-start
  6.5 13.7 %all_gather.10 = s32[64,8]{1,0:T(8,128)S(1)} all-gather(s32[8,8]{1,0:T(8,128)} %param.10), channel_id=1, replica_groups=mesh['dp'=8,'expert'=32] {'dp'}, dimensions={0}, use_global_device_ids=true | all-gather | bytes 2304 | tf_op jit(solution)/shard_map/all_gather | solution.py:45
  20.2 0.1 eq.42
  20.3 0.1 eq.38
  20.4 1.2 reduce-window.6
  21.6 0.2 slice_reduce_fusion
  21.8 0.1 fusion.24
  22.0 0.1 reduce_sum.21
  22.1 0.5 fusion.5
  22.6 13.3 %all_gather.9 = bf16[64,4096]{1,0:T(8,128)(2,1)S(1)} all-gather(bf16[8,4096]{1,0:T(8,128)(2,1)} %param.9), channel_id=1, replica_groups=mesh['dp'=8,'expert'=32] {'dp'}, dimensions={0}, use_global_device_ids=true | all-gather | bytes 589824 | tf_op jit(solution)/shard_map/all_gather | solution.py:43
  35.9 1.8 convolution_convert_fusion
  37.8 0.0 copy-start.3
  37.8 150.5 %all_to_all.10 = bf16[32,24,4096]{2,1,0:T(8,128)(2,1)S(1)} all-to-all(bf16[32,24,4096]{2,1,0:T(8,128)(2,1)S(1)} %bitcast.49), channel_id=1, replica_groups=mesh['dp'=8,'expert'=32] {'expert'}, dimensions={0} | all-to-all | bytes 12582912 | tf_op jit(solution)/shard_map/all_to_all | solution.py:51
  188.3 0.0 copy-start.1
  188.3 2.7 copy-done.1
  191.0 0.0 copy-done.3
  191.0 2.7 fusion.3
  193.7 0.0 copy-done
  193.7 12.8 %convolution_convert_fusion.1 = bf16[768,4096]{1,0:T(8,128)(2,1)} fusion(bf16[1,256,4096]{2,1,0:T(8,128)(2,1)S(1)} %copy-done, bf16[768,4096]{1,0:T(8,128)(2,1)} %bitcast.52, bf16[1,4096,256]{2,1,0:T(8,128)(2,1)} %param.13, f32[768,256]{1,0:T(8,128)} %fusion.3), kind=kOutput, calls=%fused_computation.1 | convolution fusion | flops 3225550848 | bytes 17563648 | tf_op jit(solution)/shard_map/dot_general | solution.py:11
  206.5 0.0 copy-start.2
  206.5 7.8 %all-to-all-start.1 = ((bf16[32,24,4096]{2,1,0:T(8,128)(2,1)}), bf16[32,24,4096]{2,1,0:T(8,128)(2,1)}, u32[]{:S(2)}, u32[]{:S(2)}) async-start(bf16[32,24,4096]{2,1,0:T(8,128)(2,1)} %bitcast.50), calls=%async_computation.1 | async-start | bytes 12582912 | tf_op jit(solution)/shard_map/all_to_all | solution.py:57
  214.3 0.0 reduce-scatter.2.cloned.1.call-start
  214.4 0.0 copy-done.2
  214.4 13.1 %all_gather.11 = f32[64,8]{1,0:T(8,128)S(1)} all-gather(f32[8,8]{1,0:T(8,128)S(1)} %copy-done.2), channel_id=1, replica_groups=mesh['dp'=8,'expert'=32] {'dp'}, dimensions={0}, use_global_device_ids=true | all-gather | bytes 2304 | tf_op jit(solution)/shard_map/all_gather | solution.py:46
  227.5 0.5 select_reduce_fusion
  228.0 2.1 fusion.34
  230.1 4.7 %fusion.15 = f32[64,4096]{1,0:T(8,128)} fusion(bf16[256,4096]{1,0:T(8,128)(2,1)} %param.17, bf16[64,4096]{1,0:T(8,128)(2,1)S(1)} %all_gather.9, bf16[4096,256]{1,0:T(8,128)(2,1)} %param.16, f32[64,256]{1,0:T(8,128)S(1)} %fusion.34), kind=kOutput, calls=%fused_computation.15 | convolution fusion | flops 268533760 | bytes 5832704 | tf_op jit(solution)/shard_map/dot_general | solution.py:11
  234.7 115.3 %all-to-all-done.1 = bf16[32,24,4096]{2,1,0:T(8,128)(2,1)} async-done(((bf16[32,24,4096]{2,1,0:T(8,128)(2,1)}), bf16[32,24,4096]{2,1,0:T(8,128)(2,1)}, u32[]{:S(2)}, u32[]{:S(2)}) %all-to-all-start.1) | async-done | bytes 6291488 | tf_op jit(solution)/shard_map/all_to_all | solution.py:57
  350.0 7.5 %convolution_add_fusion = f32[64,4096]{1,0:T(8,128)} fusion(f32[64,4096]{1,0:T(8,128)} %fusion.15, f32[64,768]{1,0:T(8,128)S(1)} %select_reduce_fusion, bf16[768,4096]{1,0:T(8,128)(2,1)} %bitcast.7), kind=kOutput, calls=%fused_computation.2 | convolution fusion | flops 2416181248 | bytes 8585216 | tf_op jit(solution)/shard_map/dot_general | solution.py:59
  357.5 0.0 reduce-scatter.2.cloned.1.call-update
  357.6 37.5 %reduce-scatter.2.cloned.1.call-done = f32[8,4096]{1,0:T(8,128)} async-done(((f32[64,4096]{1,0:T(8,128)}), f32[8,4096]{1,0:T(8,128)}) %reduce-scatter.2.cloned.1.call-update) | async-done | bytes 131088 | tf_op jit(solution)/shard_map/reduce_scatter | solution.py:65
  395.1 1.5 convert_element_type.30
  (4 shorter events, 0.1 us)
Async XLA Ops:
  6.5 187.2 %copy-start = (bf16[1,256,4096]{2,1,0:T(8,128)(2,1)S(1)}, bf16[1,256,4096]{2,1,0:T(8,128)(2,1)}, u32[]{:S(2)}) copy-start(bf16[1,256,4096]{2,1,0:T(8,128)(2,1)} %param.14) | copy-start | bytes 6291460
  37.8 153.2 %copy-start.3 = (bf16[1,4096,256]{2,1,0:T(8,128)(2,1)S(1)}, bf16[1,4096,256]{2,1,0:T(8,128)(2,1)}, u32[]{:S(2)}) copy-start(bf16[1,4096,256]{2,1,0:T(8,128)(2,1)} %param.12) | copy-start | bytes 6291460
  188.3 2.7 copy-start.1
  206.5 7.8 %copy-start.2 = (f32[8,8]{1,0:T(8,128)S(1)}, f32[8,8]{1,0:T(8,128)}, u32[]{:S(2)}) copy-start(f32[8,8]{1,0:T(8,128)} %param.11) | copy-start | bytes 772
  206.5 143.5 %all-to-all-start.1 = ((bf16[32,24,4096]{2,1,0:T(8,128)(2,1)}), bf16[32,24,4096]{2,1,0:T(8,128)(2,1)}, u32[]{:S(2)}, u32[]{:S(2)}) async-start(bf16[32,24,4096]{2,1,0:T(8,128)(2,1)} %bitcast.50), calls=%async_computation.1 | async-start | bytes 12582912 | tf_op jit(solution)/shard_map/all_to_all | solution.py:57
  214.3 180.8 %reduce-scatter.2.cloned.1.call-start = ((), (), s32[]{:S(2)}) async-start(), calls=%async_computation.3 | async-start | bytes 1179648 | tf_op jit(solution)/shard_map/reduce_scatter | solution.py:65
Sparse Core Ops, SparseCore 0:
  357.7 37.3 reduce-scatter.1
where the time goes:
time: 404 us; the launch traced here: 403 us
  blocking collectives  191 us (47%)
  waiting for transfers between devices  153 us (38%)
  matrix products  31.6 us (8%)
  between operations  13.5 us (3%)
  starting transfers between devices  7.82 us (2%)
    all_to_all x1, blocking collectives, per_device(): lax.all_to_all(outgoing, 'expert', split_axis=0, concat_axis=0, tiled=True)  151 us
    all_to_all x1, waiting for transfers between devices, per_device(): lax.all_to_all(partial_value, 'expert', split_axis=0, concat_axis=0, tile...  115 us
    reduce_scatter x1, waiting for transfers between devices, per_device(): lax.psum_scatter(swiglu(column, s_gate, s_up, s_down) + routed, 'dp', sca...  37.5 us
    dot_general x2, matrix products, swiglu(): return jnp.dot(hidden, down_w, preferred_element_type=jnp.float32)  17.5 us
    all_gather x1, blocking collectives, per_device(): lax.all_gather(expert_ids, 'dp', axis=0, tiled=True)  13.7 us
    all_gather x1, blocking collectives, per_device(): column = lax.all_gather(tokens, 'dp', axis=0, tiled=True)  13.3 us
    all_gather x1, blocking collectives, per_device(): lax.all_gather(gate_values, 'dp', axis=0, tiled=True)  13.1 us
  transfers between devices with their start and end apart: 2, of which 2 were waited for; matrix products, arithmetic and copies ran while one was open for 2% of the time, Pallas kernels for 0%

commit v1 on v0

--- a/solution.py
+++ b/solution.py
@@ -41,9 +41,15 @@
     up_local = w_up[0]
     down_local = w_down[0]
     column = lax.all_gather(tokens, "dp", axis=0, tiled=True)
+
+    def manage_sheets(t0, a_name):
+        return jnp.concatenate(
+            jax.lax.all_to_all(jnp.stack([t0] * jax.lax.axis_size(a_name)), a_name, 0, 0), axis=0
+        )
+
     column_ids, column_gates = (
         lax.all_gather(expert_ids, "dp", axis=0, tiled=True),
-        lax.all_gather(gate_values, "dp", axis=0, tiled=True),
+        manage_sheets(gate_values, "dp"),
     )
     column_cap = capacity * groups
     picker, combiner = slot_tables(column_ids, column_gates, experts, column_cap)

time: 404 us -> 411 us (1.017)
  waiting for transfers between devices: 153 us -> 169 us
  blocking collectives: 191 us -> 177 us
    all_to_all x1, waiting for transfers between devices: 115 us -> 134 us  [per_device(): lax.all_to_all(partial_value, 'expert', split_axis=0, concat_axis=0, tile...]
    all_gather x1 -> x0, blocking collectives: 13.1 us -> none  [per_device(): lax.all_gather(gate_values, 'dp', axis=0, tiled=True)]
  transfers between devices with their start and end apart: 2 -> 3, of which waited for: 2 -> 2; matrix products, arithmetic and copies ran while one was open for 2% -> 6% of each run, Pallas kernels for 0% -> 0%
where the time goes in v1:
time: 411 us
  blocking collectives  177 us (43%)
  waiting for transfers between devices  169 us (41%)
  matrix products  33.9 us (8%)
  between operations  13.5 us (3%)
  starting transfers between devices  11.6 us (3%)
    all_to_all x1, blocking collectives, per_device(): lax.all_to_all(outgoing, 'expert', split_axis=0, concat_axis=0, tiled=True)  150 us
    all_to_all x1, waiting for transfers between devices, per_device(): lax.all_to_all(partial_value, 'expert', split_axis=0, concat_axis=0, tile...  134 us
    reduce_scatter x1, waiting for transfers between devices, per_device(): lax.psum_scatter(swiglu(column, s_gate, s_up, s_down) + routed, 'dp', sca...  35.2 us
    dot_general x2, matrix products, swiglu(): return jnp.dot(hidden, down_w, preferred_element_type=jnp.float32)  17.3 us
    all_gather x1, blocking collectives, per_device(): lax.all_gather(expert_ids, 'dp', axis=0, tiled=True)  13.7 us
    all_gather x1, blocking collectives, per_device(): column = lax.all_gather(tokens, 'dp', axis=0, tiled=True)  13.3 us
  transfers between devices with their start and end apart: 3, of which 2 were waited for; matrix products, arithmetic and copies ran while one was open for 6% of the time, Pallas kernels for 0%

profile of v1, /device:TPU:2, one launch (start us, length us, event | category | flops | bytes accessed | tf_op | source)
XLA Modules:
  0.0 410.8 jit_solution(11360459642267480112)
XLA Ops:
  6.5 0.0 copy-start
  6.5 13.7 %all_gather.7 = s32[64,8]{1,0:T(8,128)S(1)} all-gather(s32[8,8]{1,0:T(8,128)} %param.10), channel_id=1, replica_groups=mesh['dp'=8,'expert'=32] {'dp'}, dimensions={0}, use_global_device_ids=true | all-gather | bytes 2304 | tf_op jit(solution)/shard_map/all_gather | solution.py:51
  20.2 0.1 eq.42
  20.3 0.1 eq.38
  20.4 1.2 reduce-window.6
  21.6 0.2 slice_reduce_fusion
  21.8 0.1 fusion.24
  22.0 0.1 reduce_sum.21
  22.1 0.5 fusion.5
  22.6 13.3 %all_gather.6 = bf16[64,4096]{1,0:T(8,128)(2,1)S(1)} all-gather(bf16[8,4096]{1,0:T(8,128)(2,1)} %param.9), channel_id=1, replica_groups=mesh['dp'=8,'expert'=32] {'dp'}, dimensions={0}, use_global_device_ids=true | all-gather | bytes 589824 | tf_op jit(solution)/shard_map/all_gather | solution.py:43
  35.9 1.8 convolution_convert_fusion
  37.8 0.0 copy-start.1
  37.8 150.5 %all_to_all.15 = bf16[32,24,4096]{2,1,0:T(8,128)(2,1)} all-to-all(bf16[32,24,4096]{2,1,0:T(8,128)(2,1)S(1)} %bitcast.50), channel_id=1, replica_groups=mesh['dp'=8,'expert'=32] {'expert'}, dimensions={0} | all-to-all | bytes 12582912 | tf_op jit(solution)/shard_map/all_to_all | solution.py:57
  188.3 0.0 copy-done.1
  188.3 0.6 stack.2
  188.9 3.7 all-to-all-start
  192.6 5.2 %fusion.3 = f32[768,256]{1,0:T(8,128)S(1)} fusion(bf16[768,4096]{1,0:T(8,128)(2,1)} %bitcast.52, bf16[1,4096,256]{2,1,0:T(8,128)(2,1)} %param.12), kind=kOutput, calls=%fused_computation.6 | convolution fusion | flops 1610612736 | bytes 9175040 | tf_op jit(solution)/shard_map/dot_general | solution.py:8
  197.9 0.0 copy-done
  197.9 12.7 %convolution_convert_fusion.1 = bf16[768,4096]{1,0:T(8,128)(2,1)} fusion(bf16[1,256,4096]{2,1,0:T(8,128)(2,1)S(1)} %copy-done, bf16[768,4096]{1,0:T(8,128)(2,1)} %bitcast.53, bf16[1,4096,256]{2,1,0:T(8,128)(2,1)} %param.13, f32[768,256]{1,0:T(8,128)S(1)} %fusion.3), kind=kOutput, calls=%fused_computation.1 | convolution fusion | flops 3225550848 | bytes 17563648 | tf_op jit(solution)/shard_map/dot_general | solution.py:11
  210.5 0.0 all-to-all-done
  210.5 7.6 %all-to-all-start.2 = ((bf16[32,24,4096]{2,1,0:T(8,128)(2,1)}), bf16[32,24,4096]{2,1,0:T(8,128)(2,1)}, u32[]{:S(2)}, u32[]{:S(2)}) async-start(bf16[32,24,4096]{2,1,0:T(8,128)(2,1)} %bitcast.51), calls=%async_computation.2 | async-start | bytes 12582912 | tf_op jit(solution)/shard_map/all_to_all | solution.py:63
  218.2 0.2 reduce-scatter.2.cloned.1.call-start
  218.4 2.1 fusion.34
  220.5 4.7 %fusion.15 = f32[64,4096]{1,0:T(8,128)} fusion(bf16[256,4096]{1,0:T(8,128)(2,1)} %param.17, bf16[64,4096]{1,0:T(8,128)(2,1)S(1)} %all_gather.6, bf16[4096,256]{1,0:T(8,128)(2,1)} %param.16, f32[64,256]{1,0:T(8,128)S(1)} %fusion.34), kind=kOutput, calls=%fused_computation.15 | convolution fusion | flops 268533760 | bytes 5832704 | tf_op jit(solution)/shard_map/dot_general | solution.py:11
  225.1 0.5 select_reduce_fusion
  225.7 134.1 %all-to-all-done.2 = bf16[32,24,4096]{2,1,0:T(8,128)(2,1)} async-done(((bf16[32,24,4096]{2,1,0:T(8,128)(2,1)}), bf16[32,24,4096]{2,1,0:T(8,128)(2,1)}, u32[]{:S(2)}, u32[]{:S(2)}) %all-to-all-start.2) | async-done | bytes 6291488 | tf_op jit(solution)/shard_map/all_to_all | solution.py:63
  359.8 7.5 %convolution_add_fusion = f32[64,4096]{1,0:T(8,128)} fusion(f32[64,4096]{1,0:T(8,128)} %fusion.15, f32[64,768]{1,0:T(8,128)S(1)} %select_reduce_fusion, bf16[768,4096]{1,0:T(8,128)(2,1)} %bitcast.8), kind=kOutput, calls=%fused_computation.2 | convolution fusion | flops 2416181248 | bytes 8585216 | tf_op jit(solution)/shard_map/dot_general | solution.py:65
  367.2 0.0 reduce-scatter.2.cloned.1.call-update
  367.3 35.2 %reduce-scatter.2.cloned.1.call-done = f32[8,4096]{1,0:T(8,128)} async-done(((f32[64,4096]{1,0:T(8,128)}), f32[8,4096]{1,0:T(8,128)}) %reduce-scatter.2.cloned.1.call-update) | async-done | bytes 131088 | tf_op jit(solution)/shard_map/reduce_scatter | solution.py:71
  402.4 1.5 convert_element_type.30
  (4 shorter events, 0.1 us)
Async XLA Ops:
  6.5 191.3 %copy-start = (bf16[1,256,4096]{2,1,0:T(8,128)(2,1)S(1)}, bf16[1,256,4096]{2,1,0:T(8,128)(2,1)}, u32[]{:S(2)}) copy-start(bf16[1,256,4096]{2,1,0:T(8,128)(2,1)} %param.14) | copy-start | bytes 6291460
  37.8 150.5 %copy-start.1 = (f32[8,8]{1,0:T(8,128)S(1)}, f32[8,8]{1,0:T(8,128)}, u32[]{:S(2)}) copy-start(f32[8,8]{1,0:T(8,128)} %param.11) | copy-start | bytes 772
  188.9 21.6 %all-to-all-start = ((f32[8,8,8]{2,1,0:T(8,128)}), f32[8,8,8]{2,1,0:T(8,128)S(1)}, u32[]{:S(2)}, u32[]{:S(2)}) async-start(f32[8,8,8]{2,1,0:T(8,128)} %stack.2), calls=%async_computation | async-start | bytes 65536 | tf_op jit(solution)/shard_map/all_to_all | solution.py:47
  210.5 149.2 %all-to-all-start.2 = ((bf16[32,24,4096]{2,1,0:T(8,128)(2,1)}), bf16[32,24,4096]{2,1,0:T(8,128)(2,1)}, u32[]{:S(2)}, u32[]{:S(2)}) async-start(bf16[32,24,4096]{2,1,0:T(8,128)(2,1)} %bitcast.51), calls=%async_computation.2 | async-start | bytes 12582912 | tf_op jit(solution)/shard_map/all_to_all | solution.py:63
  218.2 184.3 %reduce-scatter.2.cloned.1.call-start = ((), (), s32[]{:S(2)}) async-start(), calls=%async_computation.4 | async-start | bytes 1179648 | tf_op jit(solution)/shard_map/reduce_scatter | solution.py:71
Sparse Core Ops, SparseCore 0:
  367.4 35.0 reduce-scatter.1
